TPU v7x, 256 devices: a whole 4x4x8 slice. The times are simulated.
256 devices in a mesh: ctx: 8 (over x, core), tp: 32 (over y, z).
Axes of the slice: x: 4, y: 4, z: 8, core: 2. Of those that a mesh axis runs over, the one named last changes fastest.
Arguments:
- tokens: bfloat16 [1024, 8192], P('ctx', 'tp'), may hold values from -6 to 6
- in_weight: bfloat16 [8192, 3, 8192], P(None, None, 'tp'), may hold values from -0.0625 to 0.0625
- filter_taps: float32 [3, 3, 8192], P(None, None, 'tp'), may hold values from -2.4 to 2.4
- decay_rate: float32 [16, 8192], P(None, 'tp'), may hold values from 0.0001953125 to 0.08, as said below
- residue: float32 [16, 8192], P(None, 'tp'), may hold values from -80 to 80
Outputs:
- gated: bfloat16 [1024, 8192], P('ctx', 'tp')
Inputs may be any that keep to these rules, and one draw needn't show every extreme that they name: `decay_rate`: every decay rate lies between 0.2 / 1024 and 0.08.
All inputs are finite; a program needn't handle non-finite values.
Results may differ from a plain program's by a relative error of at most 0.015.
Values may be sent and summed in bfloat16 or wider, within the bound.
A program may use at most 128 MiB of HBM per device.

v0:
```python
import jax
import jax.numpy as jnp
from jax import lax
from jax.sharding import PartitionSpec as P

BLOCK = 128


def passed_along(value, axis, steps):
    count = lax.axis_size(axis)
    first, last = (max(0, -steps), min(count, count - steps))
    return lax.ppermute(value, axis, [(source, source + steps) for source in range(first, last)])


def entering(value, axis, join, neutral):
    count, mine = (lax.axis_size(axis), lax.axis_index(axis))
    pieces = jax.tree.map(lambda part: lax.all_gather(part, axis), value)
    total = jax.tree.map(
        lambda part, zero: jnp.full_like(part, 0) + jnp.asarray(zero, part.dtype), value, neutral
    )

    def step(position, total):
        longer = join(total, jax.tree.map(lambda part: part[position], pieces))
        return jax.tree.map(lambda new, old: jnp.where(position < mine, new, old), longer, total)

    return lax.fori_loop(0, count - 1, step, total)


def project(row_block, in_weight):
    weight_flat = in_weight.reshape(in_weight.shape[0], -1)
    gathered = lax.all_gather(row_block, "tp", axis=1, tiled=True)
    summed = jnp.dot(gathered, weight_flat, preferred_element_type=jnp.float32)
    return summed.astype(jnp.bfloat16).reshape(row_block.shape[0], 3, -1)


def combine_modes(earlier, later):
    return (earlier[0] * later[0], later[0] * earlier[1] + later[1])


def on_device(tokens, in_weight, filter_taps, decay_rate, residue):
    row_count = tokens.shape[0]
    lead_rows = filter_taps.shape[0] - 1
    projected = project(tokens, in_weight)
    rim_rows = passed_along(projected[row_count - lead_rows :], "ctx", 1)
    padded = jnp.concatenate([rim_rows, projected], axis=0)
    features = jnp.zeros((row_count,) + padded.shape[1:], jnp.float32)
    for lag_index in range(lead_rows + 1):
        window = padded[lead_rows - lag_index : lead_rows - lag_index + row_count].astype(
            jnp.float32
        )
        features = features + filter_taps[lag_index] * window
    query_part = features[:, 0]
    source = features[:, 1] * features[:, 2]
    chan_count = source.shape[1]
    block_count = row_count // BLOCK
    coeffs = residue * jnp.sqrt(1.0 - jnp.exp(-2.0 * decay_rate))
    offsets = jnp.arange(BLOCK, dtype=jnp.float32)
    falling = jnp.exp(-decay_rate[None] * offsets[:, None, None])
    rising = jnp.exp(decay_rate[None] * offsets[:, None, None])
    toeplitz = jnp.einsum(
        "inc,jnc->ijc", falling * coeffs[None], rising, precision=lax.Precision.HIGHEST
    )
    lower_mask = (offsets[:, None] >= offsets[None, :])[:, :, None]
    toeplitz = jnp.where(lower_mask, toeplitz, 0.0)
    blocks = source.reshape(block_count, BLOCK, chan_count)
    inner_part = jnp.einsum("ijc,bjc->bic", toeplitz, blocks, precision=lax.Precision.HIGHEST)
    end_weights = falling[::-1]
    partial_states = jnp.einsum(
        "jnc,bjc->bnc", end_weights, blocks, precision=lax.Precision.HIGHEST
    )
    block_decay = jnp.exp(-decay_rate * BLOCK)

    def advance(carry_state, block_term):
        return (block_decay * carry_state + block_term, carry_state)

    local_end, local_starts = lax.scan(advance, jnp.zeros_like(block_decay), partial_states)
    device_decay = jnp.exp(-decay_rate * row_count)
    identity = (jnp.ones_like(local_end), jnp.zeros_like(local_end))
    prefix = entering((device_decay, local_end), "ctx", combine_modes, identity)
    incoming = prefix[1]
    start_offsets = jnp.arange(block_count, dtype=jnp.float32) * BLOCK
    start_states = (
        local_starts + jnp.exp(-decay_rate[None] * start_offsets[:, None, None]) * incoming[None]
    )
    read_weights = coeffs[None] * jnp.exp(-decay_rate[None] * (offsets + 1.0)[:, None, None])
    carried = jnp.einsum(
        "inc,bnc->bic", read_weights, start_states, precision=lax.Precision.HIGHEST
    )
    response = (inner_part + carried).reshape(row_count, chan_count)
    return (query_part * response).astype(jnp.bfloat16)


def solution(mesh):
    return jax.shard_map(
        on_device,
        mesh=mesh,
        in_specs=(
            P("ctx", "tp"),
            P(None, None, "tp"),
            P(None, None, "tp"),
            P(None, "tp"),
            P(None, "tp"),
        ),
        out_specs=P("ctx", "tp"),
        check_vma=False,
    )
```

profile of v0, /device:TPU:1, one launch (start us, length us, event | category | flops | bytes accessed | tf_op | source)
XLA Modules:
  0.0 242.4 jit_solution(11823663511975442552)
XLA Ops:
  6.5 0.0 all-gather.4.cloned.1.call-start
  6.5 0.7 all-gather.4.cloned.1.call-update
  7.3 0.0 copy-start
  7.3 0.0 copy-start.2
  7.3 16.7 %copy.9 = bf16[8192,3,256]{0,2,1:T(8,128)(2,1)} copy(bf16[8192,3,256]{2,0,1:T(8,128)(2,1)} %param.8) | data formatting | bytes 25165824 | tf_op args[1]
  24.0 0.0 copy-done
  24.0 0.0 copy-done.2
  24.0 1.6 multiply_exponential_fusion.1
  25.6 1.6 multiply_exponential_fusion
  27.2 58.1 %all-gather.4.cloned.1.call-done = bf16[128,8192]{1,0:T(8,128)(2,1)} async-done(((bf16[128,256]{1,0:T(8,128)(2,1)}), bf16[128,8192]{1,0:T(8,128)(2,1)}) %all-gather.4.cloned.1.call-update) | async-done | bytes 2097168 | tf_op jit(solution)/shard_map/all_gather | solution.py:31
  85.4 9.5 %convolution_convert_fusion = bf16[128,768]{1,0:T(8,128)(2,1)S(1)} fusion(bf16[128,8192]{1,0:T(8,128)(2,1)} %all-gather.4.cloned.1.call-done, bf16[8192,768]{0,1:T(8,128)(2,1)} %bitcast.64), kind=kOutput, calls=%fused_computation.8 | convolution fusion | flops 1610711040 | bytes 14876672 | tf_op jit(solution)/shard_map/dot_general | solution.py:32
  94.9 0.2 copy.32
  95.1 6.6 %collective-permute-start = (bf16[2,3,256]{0,2,1:T(8,128)(2,1)S(1)}, bf16[2,3,256]{0,2,1:T(8,128)(2,1)S(1)}, u32[]{:S(2)}, u32[]{:S(2)}) collective-permute-start(bf16[2,3,256]{0,2,1:T(8,128)(2,1)S(1)} %bitcast.70), channel_id=1, source_target_pairs={{0,32},{32,64},{64,96},{96,128},{128,160},{160,192},{192,224},{1,3... | collective-permute-start | bytes 9224 | tf_op jit(solution)/shard_map/ppermute | solution.py:12
  101.7 2.5 %copy.13 = f32[128,16,256]{0,1,2:T(8,128)S(1)} copy(f32[128,16,256]{2,1,0:T(8,128)} %multiply_exponential_fusion.1) | data formatting | bytes 4194304 | tf_op jit(solution)/shard_map/exp | solution.py:59
  104.3 0.2 copy.10
  104.4 0.0 collective-permute-done
  104.4 0.5 multiply_add_fusion
  105.0 0.0 copy-start.1
  105.0 0.1 copy.33
  105.1 1.8 multiply_reduce_fusion.1
  107.0 14.2 %all-gather = f32[128,256]{1,0:T(8,128)S(1)} all-gather(f32[16,256]{1,0:T(8,128)S(1)} %get-tuple-element.146), channel_id=2, replica_groups=mesh['ctx'=8,'tp'=32] {'ctx'}, dimensions={0}, use_global_device_ids=true | all-gather | bytes 147456 | tf_op jit(solution)/shard_map/all_gather | solution.py:17
  121.1 12.9 %all-gather.1 = f32[128,256]{1,0:T(8,128)S(1)} all-gather(f32[16,256]{1,0:T(8,128)S(1)} %get-tuple-element.145), channel_id=3, replica_groups=mesh['ctx'=8,'tp'=32] {'ctx'}, dimensions={0}, use_global_device_ids=true | all-gather | bytes 147456 | tf_op jit(solution)/shard_map/all_gather | solution.py:17
  134.1 0.3 while.9
  134.3 0.0 copy-done.1
  134.4 1.6 broadcast_multiply_fusion
  136.0 0.7 multiply_reduce_fusion
  136.7 0.1 copy.31
  136.8 3.4 %copy.14 = f32[128,16,256]{0,1,2:T(8,128)} copy(f32[128,16,256]{2,1,0:T(8,128)} %broadcast_multiply_fusion) | data formatting | bytes 4194304 | tf_op jit(solution)/shard_map/mul | solution.py:61
  140.1 29.8 %fusion.4 = f32[256,128,128]{2,1,0:T(8,128)} fusion(f32[128,16,256]{0,1,2:T(8,128)S(1)} %copy.13, f32[128,16,256]{0,1,2:T(8,128)} %copy.14), kind=kOutput, calls=%fused_computation.28 | convolution fusion | flops 805306368 | bytes 20971520 | tf_op jit(solution)/shard_map/inc,jnc->ijc/dot_general | solution.py:60
  169.9 17.8 %copy.15 = f32[256,128,128]{0,1,2:T(8,128)} copy(f32[256,128,128]{2,1,0:T(8,128)} %fusion.4) | data formatting | bytes 33554432 | tf_op jit(solution)/shard_map/inc,jnc->ijc/dot_general | solution.py:60
  187.7 12.2 %bitcast_select_fusion = f32[128,128,256]{2,1,0:T(8,128)} fusion(f32[256,128,128]{0,1,2:T(8,128)} %copy.15, pred[128,128]{1,0:T(8,128)(4,1)S(1)} %iota_compare_fusion), kind=kLoop, calls=%fused_computation.3 | loop fusion | flops 4194304 | bytes 33570816 | tf_op jit(solution)/shard_map/jit(_where)/select_n | solution.py:64
  199.9 18.3 %copy.17 = f32[128,128,256]{0,1,2:T(8,128)} copy(f32[128,128,256]{2,1,0:T(8,128)} %bitcast_select_fusion) | data formatting | bytes 33554432 | tf_op jit(solution)/shard_map/jit(_where)/select_n | solution.py:64
  218.2 16.6 %fusion.5 = f32[256,1,128]{2,1,0:T(1,128)S(1)} fusion(f32[128,256,1]{0,2,1:T(1,128)S(1)} %bitcast.66, f32[128,128,256]{0,1,2:T(8,128)} %copy.17), kind=kOutput, calls=%fused_computation.29 | convolution fusion | flops 50331648 | bytes 17039360 | tf_op jit(solution)/shard_map/ijc,bjc->bic/dot_general | solution.py:66
  234.8 0.7 copy.12
  (18 shorter events, 0.2 us)
Async XLA Ops:
  6.5 78.8 %all-gather.4.cloned.1.call-start = ((), (), s32[]{:S(2)}) async-start(), calls=%async_computation | async-start | bytes 2162688 | tf_op jit(solution)/shard_map/all_gather | solution.py:31
  7.3 16.7 %copy-start = (f32[16,256]{1,0:T(8,128)S(1)}, f32[16,256]{1,0:T(8,128)}, u32[]{:S(2)}) copy-start(f32[16,256]{1,0:T(8,128)} %param.10) | copy-start | bytes 49156
  7.3 16.7 %copy-start.2 = (f32[3,3,256]{2,1,0:T(4,128)S(1)}, f32[3,3,256]{2,1,0:T(4,128)}, u32[]{:S(2)}) copy-start(f32[3,3,256]{2,1,0:T(4,128)} %param.9) | copy-start | bytes 27652
  95.1 9.4 %collective-permute-start = (bf16[2,3,256]{0,2,1:T(8,128)(2,1)S(1)}, bf16[2,3,256]{0,2,1:T(8,128)(2,1)S(1)}, u32[]{:S(2)}, u32[]{:S(2)}) collective-permute-start(bf16[2,3,256]{0,2,1:T(8,128)(2,1)S(1)} %bitcast.70), channel_id=1, source_target_pairs={{0,32},{32,64},{64,96},{96,128},{128,160},{160,192},{192,224},{1,3... | collective-permute-start | bytes 9224 | tf_op jit(solution)/shard_map/ppermute | solution.py:12
  105.0 29.3 %copy-start.1 = (f32[16,256]{1,0:T(8,128)S(1)}, f32[16,256]{1,0:T(8,128)}, u32[]{:S(2)}) copy-start(f32[16,256]{1,0:T(8,128)} %param.11) | copy-start | bytes 49156
Sparse Core Ops, SparseCore 0:
  9.8 75.4 all-gather.3
where the time goes:
time: 243 us; the launch traced here: 242 us
  local copies, waits for them, and re-layouts  60 us (25%)
  waiting for transfers between devices  58.8 us (24%)
  matrix products  55.8 us (23%)
  blocking collectives  27.1 us (11%)
  other arithmetic  20.3 us (8%)
  between operations  13.6 us (6%)
  starting transfers between devices  6.64 us (3%)
    all_gather x1, waiting for transfers between devices, project(): gathered = lax.all_gather(row_block, 'tp', axis=1, tiled=True)  58.1 us
    dot_general x1, matrix products, on_device(): jnp.einsum('inc,jnc->ijc', falling * coeffs[None], rising, precision=lax....  29.8 us
    all_gather x2, blocking collectives, entering(): pieces = jax.tree.map(lambda part: lax.all_gather(part, axis), value)  27.1 us
    select_n x1, local copies, waits for them, and re-layouts, on_device(): toeplitz = jnp.where(lower_mask, toeplitz, 0.0)  18.3 us
    dot_general x1, local copies, waits for them, and re-layouts, on_device(): jnp.einsum('inc,jnc->ijc', falling * coeffs[None], rising, precision=lax....  17.8 us
    unnamed x8, local copies, waits for them, and re-layouts  16.8 us
    dot_general x1, matrix products, on_device(): jnp.einsum('ijc,bjc->bic', toeplitz, blocks, precision=lax.Precision.HIGH...  16.6 us
    select_n x1, other arithmetic, on_device(): toeplitz = jnp.where(lower_mask, toeplitz, 0.0)  12.2 us
  transfers between devices with their start and end apart: 2, of which 1 were waited for; matrix products, arithmetic and copies ran while one was open for 9% of the time, Pallas kernels for 0%

commit v1 on v0

--- a/solution.py
+++ b/solution.py
@@ -28,7 +28,9 @@
 
 def project(row_block, in_weight):
     weight_flat = in_weight.reshape(in_weight.shape[0], -1)
-    gathered = lax.all_gather(row_block, "tp", axis=1, tiled=True)
+    gathered = jnp.concatenate(
+        lax.all_to_all(jnp.stack([row_block] * lax.axis_size("tp")), "tp", 0, 0), axis=1
+    )
     summed = jnp.dot(gathered, weight_flat, preferred_element_type=jnp.float32)
     return summed.astype(jnp.bfloat16).reshape(row_block.shape[0], 3, -1)
 

time: 243 us -> 213 us (0.88)
  waiting for transfers between devices: 58.8 us -> 28.9 us
  between operations: 13.6 us -> 0.21 us
  starting transfers between devices: 6.64 us -> 17.1 us
  local copies, waits for them, and re-layouts: 60 us -> 62.8 us
    all_gather x1 -> x0, waiting for transfers between devices: 58.1 us -> none  [project(): gathered = lax.all_gather(row_block, 'tp', axis=1, tiled=True)]
    all_to_all x0 -> x1, waiting for transfers between devices: none -> 28.9 us  [project(): lax.all_to_all(jnp.stack([row_block] * lax.axis_size('tp')), 'tp', 0, 0)]
    all_to_all x0 -> x1, starting transfers between devices: none -> 12 us  [project(): lax.all_to_all(jnp.stack([row_block] * lax.axis_size('tp')), 'tp', 0, 0)]
    unnamed x8 -> x9, local copies, waits for them, and re-layouts: 16.8 us -> 17.8 us
  transfers between devices with their start and end apart: 2 -> 2, of which waited for: 1 -> 1; matrix products, arithmetic and copies ran while one was open for 9% -> 11% of each run, Pallas kernels for 0% -> 0%
where the time goes in v1:
time: 213 us; the launch traced here: 212 us
  local copies, waits for them, and re-layouts  62.8 us (29%)
  matrix products  55.2 us (26%)
  waiting for transfers between devices  28.9 us (14%)
  blocking collectives  27.1 us (13%)
  other arithmetic  20.3 us (10%)
  starting transfers between devices  17.1 us (8%)
    dot_general x1, matrix products, on_device(): jnp.einsum('inc,jnc->ijc', falling * coeffs[None], rising, precision=lax....  29.8 us
    all_to_all x1, waiting for transfers between devices, project(): lax.all_to_all(jnp.stack([row_block] * lax.axis_size('tp')), 'tp', 0, 0)  28.9 us
    all_gather x2, blocking collectives, entering(): pieces = jax.tree.map(lambda part: lax.all_gather(part, axis), value)  27.1 us
    select_n x1, local copies, waits for them, and re-layouts, on_device(): toeplitz = jnp.where(lower_mask, toeplitz, 0.0)  18.3 us
    unnamed x9, local copies, waits for them, and re-layouts  17.8 us
    dot_general x1, local copies, waits for them, and re-layouts, on_device(): jnp.einsum('inc,jnc->ijc', falling * coeffs[None], rising, precision=lax....  17.8 us
    dot_general x1, matrix products, on_device(): jnp.einsum('ijc,bjc->bic', toeplitz, blocks, precision=lax.Precision.HIGH...  16.6 us
    select_n x1, other arithmetic, on_device(): toeplitz = jnp.where(lower_mask, toeplitz, 0.0)  12.2 us
  transfers between devices with their start and end apart: 2, of which 1 were waited for; matrix products, arithmetic and copies ran while one was open for 11% of the time, Pallas kernels for 0%

profile of v1, /device:TPU:1, one launch (start us, length us, event | category | flops | bytes accessed | tf_op | source)
XLA Modules:
  0.0 211.8 jit_solution(13360768212696764891)
XLA Ops:
  0.0 0.9 copy.9
  1.0 1.8 stack.2
  2.8 12.0 %all-to-all-start = ((bf16[32,128,256]{1,2,0:T(8,128)(2,1)}), bf16[32,128,256]{1,2,0:T(8,128)(2,1)S(1)}, u32[]{:S(2)}, u32[]{:S(2)}) async-start(bf16[32,128,256]{1,2,0:T(8,128)(2,1)} %stack.2), calls=%async_computation | async-start | bytes 4194304 | tf_op jit(solution)/shard_map/all_to_all | solution.py:32
  14.8 0.0 copy-start
  14.8 0.0 copy-start.2
  14.8 16.7 %copy.10 = bf16[8192,3,256]{0,2,1:T(8,128)(2,1)} copy(bf16[8192,3,256]{2,0,1:T(8,128)(2,1)} %param.8) | data formatting | bytes 25165824 | tf_op args[1]
  31.6 0.0 copy-done
  31.6 0.0 copy-done.2
  31.6 1.6 multiply_exponential_fusion.1
  33.2 1.6 multiply_exponential_fusion
  34.8 28.9 %all-to-all-done = bf16[32,128,256]{1,2,0:T(8,128)(2,1)S(1)} async-done(((bf16[32,128,256]{1,2,0:T(8,128)(2,1)}), bf16[32,128,256]{1,2,0:T(8,128)(2,1)S(1)}, u32[]{:S(2)}, u32[]{:S(2)}) %all-to-all-start) | async-done | bytes 2097184 | tf_op jit(solution)/shard_map/all_to_all | solution.py:32
  63.7 8.9 %convolution_convert_fusion = bf16[128,768]{1,0:T(8,128)(2,1)S(1)} fusion(bf16[128,8192]{0,1:T(8,128)(2,1)S(1)} %bitcast.68, bf16[8192,768]{0,1:T(8,128)(2,1)} %bitcast.67), kind=kOutput, calls=%fused_computation.8 | convolution fusion | flops 1610711040 | bytes 14876672 | tf_op jit(solution)/shard_map/dot_general | solution.py:34
  72.6 0.2 copy.33
  72.8 5.1 %collective-permute-start = (bf16[2,3,256]{0,2,1:T(8,128)(2,1)S(1)}, bf16[2,3,256]{0,2,1:T(8,128)(2,1)S(1)}, u32[]{:S(2)}, u32[]{:S(2)}) collective-permute-start(bf16[2,3,256]{0,2,1:T(8,128)(2,1)S(1)} %bitcast.74), channel_id=1, source_target_pairs={{0,32},{32,64},{64,96},{96,128},{128,160},{160,192},{192,224},{1,3... | collective-permute-start | bytes 9224 | tf_op jit(solution)/shard_map/ppermute | solution.py:12
  78.0 2.5 %copy.14 = f32[128,16,256]{0,1,2:T(8,128)S(1)} copy(f32[128,16,256]{2,1,0:T(8,128)} %multiply_exponential_fusion.1) | data formatting | bytes 4194304 | tf_op jit(solution)/shard_map/exp | solution.py:61
  80.5 0.2 copy.11
  80.6 0.0 collective-permute-done
  80.7 0.5 multiply_add_fusion
  81.2 0.0 copy-start.1
  81.2 0.1 copy.34
  81.4 1.8 multiply_reduce_fusion.1
  83.2 14.2 %all-gather = f32[128,256]{1,0:T(8,128)S(1)} all-gather(f32[16,256]{1,0:T(8,128)S(1)} %get-tuple-element.146), channel_id=2, replica_groups=mesh['ctx'=8,'tp'=32] {'ctx'}, dimensions={0}, use_global_device_ids=true | all-gather | bytes 147456 | tf_op jit(solution)/shard_map/all_gather | solution.py:17
  97.4 12.9 %all-gather.1 = f32[128,256]{1,0:T(8,128)S(1)} all-gather(f32[16,256]{1,0:T(8,128)S(1)} %get-tuple-element.145), channel_id=3, replica_groups=mesh['ctx'=8,'tp'=32] {'ctx'}, dimensions={0}, use_global_device_ids=true | all-gather | bytes 147456 | tf_op jit(solution)/shard_map/all_gather | solution.py:17
  110.3 0.3 while.9
  110.6 0.0 copy-done.1
  110.6 1.6 broadcast_multiply_fusion
  112.2 0.7 multiply_reduce_fusion
  112.9 0.1 copy.32
  113.0 3.4 %copy.15 = f32[128,16,256]{0,1,2:T(8,128)} copy(f32[128,16,256]{2,1,0:T(8,128)} %broadcast_multiply_fusion) | data formatting | bytes 4194304 | tf_op jit(solution)/shard_map/mul | solution.py:63
  116.3 29.8 %fusion.4 = f32[256,128,128]{2,1,0:T(8,128)} fusion(f32[128,16,256]{0,1,2:T(8,128)S(1)} %copy.14, f32[128,16,256]{0,1,2:T(8,128)} %copy.15), kind=kOutput, calls=%fused_computation.28 | convolution fusion | flops 805306368 | bytes 20971520 | tf_op jit(solution)/shard_map/inc,jnc->ijc/dot_general | solution.py:62
  146.1 17.8 %copy.16 = f32[256,128,128]{0,1,2:T(8,128)} copy(f32[256,128,128]{2,1,0:T(8,128)} %fusion.4) | data formatting | bytes 33554432 | tf_op jit(solution)/shard_map/inc,jnc->ijc/dot_general | solution.py:62
  163.9 12.2 %bitcast_select_fusion = f32[128,128,256]{2,1,0:T(8,128)} fusion(f32[256,128,128]{0,1,2:T(8,128)} %copy.16, pred[128,128]{1,0:T(8,128)(4,1)S(1)} %iota_compare_fusion), kind=kLoop, calls=%fused_computation.3 | loop fusion | flops 4194304 | bytes 33570816 | tf_op jit(solution)/shard_map/jit(_where)/select_n | solution.py:66
  176.1 18.3 %copy.18 = f32[128,128,256]{0,1,2:T(8,128)} copy(f32[128,128,256]{2,1,0:T(8,128)} %bitcast_select_fusion) | data formatting | bytes 33554432 | tf_op jit(solution)/shard_map/jit(_where)/select_n | solution.py:66
  194.4 16.6 %fusion.5 = f32[256,1,128]{2,1,0:T(1,128)S(1)} fusion(f32[128,256,1]{0,2,1:T(1,128)S(1)} %bitcast.70, f32[128,128,256]{0,1,2:T(8,128)} %copy.18), kind=kOutput, calls=%fused_computation.29 | convolution fusion | flops 50331648 | bytes 17039360 | tf_op jit(solution)/shard_map/ijc,bjc->bic/dot_general | solution.py:68
  211.0 0.7 copy.13
  (18 shorter events, 0.2 us)
Async XLA Ops:
  2.8 60.9 %all-to-all-start = ((bf16[32,128,256]{1,2,0:T(8,128)(2,1)}), bf16[32,128,256]{1,2,0:T(8,128)(2,1)S(1)}, u32[]{:S(2)}, u32[]{:S(2)}) async-start(bf16[32,128,256]{1,2,0:T(8,128)(2,1)} %stack.2), calls=%async_computation | async-start | bytes 4194304 | tf_op jit(solution)/shard_map/all_to_all | solution.py:32
  14.8 16.8 %copy-start = (f32[16,256]{1,0:T(8,128)S(1)}, f32[16,256]{1,0:T(8,128)}, u32[]{:S(2)}) copy-start(f32[16,256]{1,0:T(8,128)} %param.10) | copy-start | bytes 49156
  14.8 16.8 %copy-start.2 = (f32[3,3,256]{2,1,0:T(4,128)S(1)}, f32[3,3,256]{2,1,0:T(4,128)}, u32[]{:S(2)}) copy-start(f32[3,3,256]{2,1,0:T(4,128)} %param.9) | copy-start | bytes 27652
  72.8 7.8 %collective-permute-start = (bf16[2,3,256]{0,2,1:T(8,128)(2,1)S(1)}, bf16[2,3,256]{0,2,1:T(8,128)(2,1)S(1)}, u32[]{:S(2)}, u32[]{:S(2)}) collective-permute-start(bf16[2,3,256]{0,2,1:T(8,128)(2,1)S(1)} %bitcast.74), channel_id=1, source_target_pairs={{0,32},{32,64},{64,96},{96,128},{128,160},{160,192},{192,224},{1,3... | collective-permute-start | bytes 9224 | tf_op jit(solution)/shard_map/ppermute | solution.py:12
  81.2 29.4 %copy-start.1 = (f32[16,256]{1,0:T(8,128)S(1)}, f32[16,256]{1,0:T(8,128)}, u32[]{:S(2)}) copy-start(f32[16,256]{1,0:T(8,128)} %param.11) | copy-start | bytes 49156
